TPU v7x, 32 devices: a whole 2x2x4 slice. The times are simulated.
32 devices in a mesh: patch: 2 (over x), row: 4 (over y, core), col: 4 (over z).
Axes of the slice: x: 2, y: 2, z: 4, core: 2. Of those that a mesh axis runs over, the one named last changes fastest.
Arguments:
- sky_cube: float32 [512, 128, 512], P(None, ('patch', 'row'), 'col'), parts along dimension 1, may hold values from -40 to 140
- beam_taps: float32 [512, 33], replicated, may hold values from 0 to 0.2
Outputs:
- cleaned_cube: float32 [512, 128, 512], P(None, ('patch', 'row'), 'col'), parts along dimension 1
There are 2 independent parts, one for each index of `patch`. A program takes and returns all parts, laid end to end along the dimension named above; an argument that names none is the same for every part. Nothing has to cross between parts.
All inputs are finite; a program needn't handle non-finite values.
Results may differ from a plain program's by a relative error of at most 0.00085.
Values sent between devices are 32-bit elements; how exact they have to be, the bound alone decides.
No kernel may reach another device: no remote copies, remote signals or barrier semaphores. Data moves between devices by JAX's collectives and lax.ppermute only.
A program may use at most 64 MiB of HBM per device.

v0:
```python
import jax
import jax.numpy as jnp
from jax import lax
from jax.sharding import PartitionSpec as P

MODES = 4
SWEEPS = 3


def padded(array, sides, width):
    for axis, dim in sides:
        peers, length = (lax.axis_size(axis), array.shape[dim])
        up = [(i, (i + 1) % peers) for i in range(peers - 1)]
        down = [(j, i) for i, j in up]
        last = lax.slice_in_dim(array, length - width, length, axis=dim)
        leading = lax.slice_in_dim(array, 0, width, axis=dim)
        before = lax.ppermute(last, axis, up)
        after = lax.ppermute(leading, axis, down)
        array = jnp.concatenate([before, array, after], axis=dim)
    return array


def convolve(padded_field, beam_taps, axis_dim, out_width):
    result = None
    for offset in range(beam_taps.shape[1]):
        piece = lax.slice_in_dim(padded_field, offset, offset + out_width, axis=axis_dim)
        term = beam_taps[:, offset][:, None, None] * piece
        result = term if result is None else result + term
    return result


def orthonormalize(block):
    length = block.shape[0]
    columns = []
    for index in range(block.shape[1]):
        vector = block[:, index]
        for repeat in range(2):
            for earlier in columns:
                vector = vector - jnp.sum(earlier * vector) * earlier
        scale_mean = jnp.mean(vector * vector) + 1e-06
        vector = vector / jnp.sqrt(scale_mean) / jnp.sqrt(jnp.float32(length))
        columns.append(vector)
    return jnp.stack(columns, axis=1)


def leading_modes(gram_matrix, channels):
    scaled_gram = gram_matrix * (channels / jnp.trace(gram_matrix))
    channel_pos = jnp.arange(channels).astype(jnp.float32)
    mode_index = jnp.arange(MODES).astype(jnp.float32)
    cosine_basis = jnp.cos(jnp.pi * mode_index[None, :] * (channel_pos[:, None] + 0.5) / channels)
    basis = orthonormalize(cosine_basis)
    for sweep in range(SWEEPS):
        basis = orthonormalize(
            jnp.dot(
                scaled_gram,
                basis,
                precision=lax.Precision.HIGHEST,
                preferred_element_type=jnp.float32,
            )
        )
    return basis


def per_device(sky_cube, beam_taps):
    margin = beam_taps.shape[1] // 2
    channels, tile_rows, tile_cols = sky_cube.shape
    extended = padded(sky_cube, (("col", 2),), margin)
    smoothed = convolve(extended, beam_taps, 2, tile_cols)
    extended_rows = padded(smoothed, (("row", 1),), margin)
    beamed = convolve(extended_rows, beam_taps, 1, tile_rows)
    flattened = beamed.reshape(channels, tile_rows * tile_cols)
    partial_gram = jnp.dot(
        flattened, flattened.T, precision=lax.Precision.HIGHEST, preferred_element_type=jnp.float32
    )
    gram_matrix = lax.psum(partial_gram, ("row", "col"))
    mode_spectra = leading_modes(gram_matrix, channels)
    coefficients = jnp.dot(
        mode_spectra.T,
        flattened,
        precision=lax.Precision.HIGHEST,
        preferred_element_type=jnp.float32,
    )
    cleaned = flattened - jnp.dot(
        mode_spectra,
        coefficients,
        precision=lax.Precision.HIGHEST,
        preferred_element_type=jnp.float32,
    )
    return cleaned.reshape(channels, tile_rows, tile_cols)


def solution(mesh):
    placed = (P(None, ("patch", "row"), "col"), P())
    return jax.shard_map(
        per_device,
        mesh=mesh,
        in_specs=placed,
        out_specs=P(None, ("patch", "row"), "col"),
        check_vma=False,
    )
```

profile of v0, /device:TPU:0, one launch (start us, length us, event | category | flops | bytes accessed | tf_op | source)
XLA Modules:
  0.0 529.3 jit_solution(5304933710967582449)
XLA Ops:
  6.5 7.9 %fusion.232 = (f32[512,16,16]{2,1,0:T(8,128)}, f32[512,16,16]{2,1,0:T(8,128)}) fusion(f32[512,16,128]{2,1,0:T(8,128)} %param.2), kind=kLoop, calls=%fused_computation.501 | loop fusion | bytes 2097152 | tf_op jit(solution)/shard_map/slice | solution.py:15
  14.5 2.8 copy.12
  17.3 1.3 collective-permute-start.1
  18.6 2.8 copy.11
  21.4 5.6 %collective-permute-start = (f32[512,16,16]{0,2,1:T(8,128)S(1)}, f32[512,16,16]{0,2,1:T(8,128)S(1)}, u32[]{:S(2)}, u32[]{:S(2)}) collective-permute-start(f32[512,16,16]{0,2,1:T(8,128)S(1)} %copy.11), channel_id=1, source_target_pairs={{0,1},{1,2},{2,3},{4,5},{5,6},{6,7},{8,9},{9,10},{10,11},{12,13},{... | collective-permute-start | bytes 1572872 | tf_op jit(solution)/shard_map/ppermute | solution.py:17
  27.1 7.1 %collective-permute-done.1 = f32[512,16,16]{0,2,1:T(8,128)S(1)} collective-permute-done((f32[512,16,16]{0,2,1:T(8,128)S(1)}, f32[512,16,16]{0,2,1:T(8,128)S(1)}, u32[]{:S(2)}, u32[]{:S(2)}) %collective-permute-start.1) | collective-permute-done | bytes 524320 | tf_op jit(solution)/shard_map/ppermute | solution.py:18
  34.2 3.6 copy.8
  38.2 3.7 copy.6
  41.8 124.4 %fusion.91 = f32[512,16,128]{2,1,0:T(8,128)} fusion(f32[512,16,128]{2,1,0:T(8,128)} %param.2, f32[512,16,16]{2,1,0:T(8,128)} %copy.8, f32[512,16,16]{2,1,0:T(8,128)} %copy.6, f32[512]{0:T(512)S(1)} %bitcast.136, f32[512]{0:T(512)S(1)} %bitcast.138, f32[512]{0:T(512)S(1)} %bitcast.142, f32[512]{0:T(512)S(1)} %bitcast.144, f32[512]{0:T(512)S(1)} %bitcast.146, ...), kind=kLoop, calls=%fused_computation.207 | loop fusion | flops 101711872 | bytes 9504768 | tf_op jit(solution)/shard_map/add | solution.py:28
  166.3 1.3 collective-permute-start.3
  167.6 5.0 collective-permute-start.2
  187.5 114.2 %fusion.4 = f32[512,16,128]{2,1,0:T(8,128)S(1)} fusion(f32[512,16,128]{2,1,0:T(8,128)} %fusion.91, f32[512,16,128]{2,1,0:T(8,128)} %collective-permute-done.3, f32[512,16,128]{2,1,0:T(8,128)} %collective-permute-done.2, f32[512]{0:T(512)S(1)} %bitcast.137, f32[512]{0:T(512)S(1)} %bitcast.139, f32[512]{0:T(512)S(1)} %bitcast.143, f32[512]{0:T(512)S(1)} %bitcast.145, ...), kind=kLoop, calls=%fused_computation.120 | loop fusion | flops 99614720 | bytes 16844800 | tf_op jit(solution)/shard_map/add | solution.py:28
  301.7 2.0 copy-done
  303.7 10.8 %fusion.190 = f32[512,512]{1,0:T(8,128)} fusion(f32[512,16,128]{2,1,0:T(8,128)S(1)} %fusion.4), kind=kOutput, calls=%fused_computation.311 | convolution fusion | flops 6442450944 | bytes 5242880 | tf_op jit(solution)/shard_map/dot_general | solution.py:72
  318.3 123.3 %all-reduce.2.cloned.1.call-done = f32[512,512]{1,0:T(8,128)} async-done(((f32[512,512]{1,0:T(8,128)}), f32[512,512]{1,0:T(8,128)}) %all-reduce.2.cloned.1.call-update) | async-done | bytes 1048592 | tf_op jit(solution)/shard_map/psum | solution.py:75
  441.5 2.1 select_reduce_fusion
  444.3 2.2 fusion.197
  446.6 0.7 multiply_reduce_fusion.47
  452.8 0.7 multiply_reduce_fusion.42
  456.1 0.7 multiply_reduce_fusion.37
  459.3 0.7 multiply_reduce_fusion.36
  460.7 0.7 multiply_reduce_fusion.35
  463.5 0.7 multiply_reduce_fusion.33
  464.9 0.7 multiply_reduce_fusion.32
  466.3 2.2 fusion.195
  468.5 0.7 multiply_reduce_fusion.31
  474.8 0.7 multiply_reduce_fusion.26
  478.1 0.7 multiply_reduce_fusion.21
  481.3 0.7 multiply_reduce_fusion.20
  482.7 0.7 multiply_reduce_fusion.19
  485.5 0.7 multiply_reduce_fusion.17
  486.8 0.7 multiply_reduce_fusion.16
  488.3 1.0 fusion.193
  489.3 0.7 multiply_reduce_fusion.15
  490.8 0.7 multiply_reduce_fusion.14
  492.2 0.7 multiply_reduce_fusion.11
  494.1 0.7 multiply_reduce_fusion.12
  495.6 0.7 multiply_reduce_fusion.10
  497.0 0.7 multiply_reduce_fusion.6
  498.9 0.7 multiply_reduce_fusion.5
  502.1 0.7 multiply_reduce_fusion.4
  503.5 0.7 multiply_reduce_fusion.3
  504.9 0.7 multiply_reduce_fusion.2
  506.2 0.7 multiply_reduce_fusion.1
  507.6 0.7 multiply_reduce_fusion
  509.1 5.7 %fusion.180 = f32[4,2048]{1,0:T(4,128)S(1)} fusion(f32[64,8,16,128]{3,2,1,0:T(8,128)} %bitcast.86, f32[512,1]{0,1:T(1,128)S(1)} %divide_multiply_fusion, f32[512,1]{0,1:T(1,128)S(1)} %get-tuple-element.31, f32[512,1]{0,1:T(1,128)S(1)} %get-tuple-element.29, f32[512,1]{0,1:T(1,128)S(1)} %get-tuple-element.46), kind=kOutput, calls=%fused_computation.297 | convolution fusion | flops 50337792 | bytes 4235264 | tf_op jit(solution)/shard_map/dot_general | solution.py:77
  514.8 4.7 fusion.182
  519.5 2.9 copy.14
  (74 shorter events, 17.6 us)
Async XLA Ops:
  6.5 435.0 %all-reduce.2.cloned.1.call-start = ((), (), s32[]{:S(2)}) async-start(), calls=%async_computation | async-start | bytes 2097152 | tf_op jit(solution)/shard_map/psum | solution.py:75
  14.5 12.6 %copy-start.3 = (f32[512,33]{0,1:T(8,128)S(1)}, f32[512,33]{0,1:T(8,128)}, u32[]{:S(2)}) copy-start(f32[512,33]{0,1:T(8,128)} %param.3) | copy-start | bytes 202756
  17.3 16.9 %collective-permute-start.1 = (f32[512,16,16]{0,2,1:T(8,128)S(1)}, f32[512,16,16]{0,2,1:T(8,128)S(1)}, u32[]{:S(2)}, u32[]{:S(2)}) collective-permute-start(f32[512,16,16]{0,2,1:T(8,128)S(1)} %copy.12), channel_id=1, source_target_pairs={{1,0},{2,1},{3,2},{5,4},{6,5},{7,6},{9,8},{10,9},{11,10},{13,12},{... | collective-permute-start | bytes 1572872 | tf_op jit(solution)/shard_map/ppermute | solution.py:18
  21.4 16.8 %collective-permute-start = (f32[512,16,16]{0,2,1:T(8,128)S(1)}, f32[512,16,16]{0,2,1:T(8,128)S(1)}, u32[]{:S(2)}, u32[]{:S(2)}) collective-permute-start(f32[512,16,16]{0,2,1:T(8,128)S(1)} %copy.11), channel_id=1, source_target_pairs={{0,1},{1,2},{2,3},{4,5},{5,6},{6,7},{8,9},{9,10},{10,11},{12,13},{... | collective-permute-start | bytes 1572872 | tf_op jit(solution)/shard_map/ppermute | solution.py:17
  166.3 21.2 %collective-permute-start.3 = (f32[512,16,128]{2,1,0:T(8,128)}, f32[512,16,128]{2,1,0:T(8,128)}, u32[]{:S(2)}, u32[]{:S(2)}) collective-permute-start(f32[512,16,128]{2,1,0:T(8,128)} %fusion.91), channel_id=1, source_target_pairs={{4,0},{8,4},{12,8},{5,1},{9,5},{13,9},{6,2},{10,6},{14,10},{7,3},{... | collective-permute-start | bytes 12582920 | tf_op jit(solution)/shard_map/ppermute | solution.py:18
  167.6 19.9 %collective-permute-start.2 = (f32[512,16,128]{2,1,0:T(8,128)}, f32[512,16,128]{2,1,0:T(8,128)}, u32[]{:S(2)}, u32[]{:S(2)}) collective-permute-start(f32[512,16,128]{2,1,0:T(8,128)} %fusion.91), channel_id=1, source_target_pairs={{0,4},{4,8},{8,12},{1,5},{5,9},{9,13},{2,6},{6,10},{10,14},{3,7},{... | collective-permute-start | bytes 12582920 | tf_op jit(solution)/shard_map/ppermute | solution.py:17
  301.7 2.0 copy-start
  441.5 46.8 %copy-start.2 = (f32[512,512]{1,0:T(8,128)S(1)}, f32[512,512]{1,0:T(8,128)}, u32[]{:S(2)}) copy-start(f32[512,512]{1,0:T(8,128)} %all-reduce.2.cloned.1.call-done) | copy-start | bytes 3145732
  509.1 5.7 %copy-start.1 = (f32[512,16,128]{2,1,0:T(8,128)S(1)}, f32[512,16,128]{2,1,0:T(8,128)}, u32[]{:S(2)}) copy-start(f32[512,16,128]{2,1,0:T(8,128)} %copy-done) | copy-start | bytes 12582916
Sparse Core Ops, SparseCore 0:
  314.6 126.8 all-reduce.1
where the time goes:
time: 530 us; the launch traced here: 529 us
  other arithmetic  276 us (52%)
  waiting for transfers between devices  131 us (25%)
  between operations  57.1 us (11%)
  matrix products  26.6 us (5%)
  local copies, waits for them, and re-layouts  25.8 us (5%)
  starting transfers between devices  13.2 us (2%)
    add x2, other arithmetic, convolve(): result = term if result is None else result + term  239 us
    psum x1, waiting for transfers between devices, per_device(): gram_matrix = lax.psum(partial_gram, ('row', 'col'))  123 us
    reduce_sum x36, other arithmetic, orthonormalize(): vector = vector - jnp.sum(earlier * vector) * earlier  24 us
    dot_general x1, matrix products, per_device(): jnp.dot(flattened, flattened.T, precision=lax.Precision.HIGHEST, preferre...  10.8 us
    ppermute x2, starting transfers between devices, padded(): before = lax.ppermute(last, axis, up)  10.6 us
  transfers between devices with their start and end apart: 5, of which 3 were waited for; matrix products, arithmetic and copies ran while one was open for 3% of the time, Pallas kernels for 0%

commit v1 on v0

--- a/solution.py
+++ b/solution.py
@@ -72,7 +72,7 @@
     partial_gram = jnp.dot(
         flattened, flattened.T, precision=lax.Precision.HIGHEST, preferred_element_type=jnp.float32
     )
-    gram_matrix = lax.psum(partial_gram, ("row", "col"))
+    gram_matrix = jnp.sum(lax.all_gather(partial_gram, ("row", "col")), axis=0)
     mode_spectra = leading_modes(gram_matrix, channels)
     coefficients = jnp.dot(
         mode_spectra.T,

time: 530 us -> 477 us (0.900)
  other arithmetic: 276 us -> 193 us
  waiting for transfers between devices: 131 us -> 165 us
    all_gather x0 -> x1, waiting for transfers between devices: none -> 151 us  [per_device(): gram_matrix = jnp.sum(lax.all_gather(partial_gram, ('row', 'col')), axis=0)]
    psum x1 -> x0, waiting for transfers between devices: 123 us -> none  [per_device(): gram_matrix = lax.psum(partial_gram, ('row', 'col'))]
    add x2, other arithmetic: 239 us -> 149 us  [convolve(): result = term if result is None else result + term]
    reduce_sum x0 -> x1, other arithmetic: none -> 7.91 us  [per_device(): gram_matrix = jnp.sum(lax.all_gather(partial_gram, ('row', 'col')), axis=0)]
  transfers between devices with their start and end apart: 5 -> 5, of which waited for: 3 -> 5; matrix products, arithmetic and copies ran while one was open for 3% -> 3% of each run, Pallas kernels for 0% -> 0%
where the time goes in v1:
time: 477 us; the launch traced here: 476 us
  other arithmetic  193 us (40%)
  waiting for transfers between devices  165 us (35%)
  between operations  56.5 us (12%)
  local copies, waits for them, and re-layouts  25.8 us (5%)
  matrix products  24.2 us (5%)
  starting transfers between devices  11.5 us (2%)
    all_gather x1, waiting for transfers between devices, per_device(): gram_matrix = jnp.sum(lax.all_gather(partial_gram, ('row', 'col')), axis=0)  151 us
    add x2, other arithmetic, convolve(): result = term if result is None else result + term  149 us
    reduce_sum x36, other arithmetic, orthonormalize(): vector = vector - jnp.sum(earlier * vector) * earlier  24.2 us
    ppermute x2, waiting for transfers between devices, padded(): after = lax.ppermute(leading, axis, down)  11.5 us
    dot_general x1, matrix products, per_device(): jnp.dot(flattened, flattened.T, precision=lax.Precision.HIGHEST, preferre...  10.7 us
    unnamed x9, local copies, waits for them, and re-layouts  10.6 us
    reduce_sum x16, other arithmetic, orthonormalize(): scale_mean = jnp.mean(vector * vector) + 1e-06  10.6 us
  transfers between devices with their start and end apart: 5, of which 5 were waited for; matrix products, arithmetic and copies ran while one was open for 3% of the time, Pallas kernels for 0%

profile of v1, /device:TPU:0, one launch (start us, length us, event | category | flops | bytes accessed | tf_op | source)
XLA Modules:
  0.0 476.0 jit_solution(13205104775381721448)
XLA Ops:
  6.5 7.9 %fusion.232 = (f32[512,16,16]{2,1,0:T(8,128)}, f32[512,16,16]{2,1,0:T(8,128)}) fusion(f32[512,16,128]{2,1,0:T(8,128)} %param.2), kind=kLoop, calls=%fused_computation.501 | loop fusion | bytes 2097152 | tf_op jit(solution)/shard_map/slice | solution.py:15
  14.5 2.8 copy.18
  17.3 1.3 collective-permute-start.1
  18.6 2.8 copy.17
  21.4 5.6 %collective-permute-start = (f32[512,16,16]{0,2,1:T(8,128)S(1)}, f32[512,16,16]{0,2,1:T(8,128)S(1)}, u32[]{:S(2)}, u32[]{:S(2)}) collective-permute-start(f32[512,16,16]{0,2,1:T(8,128)S(1)} %copy.17), channel_id=1, source_target_pairs={{0,1},{1,2},{2,3},{4,5},{5,6},{6,7},{8,9},{9,10},{10,11},{12,13},{... | collective-permute-start | bytes 1572872 | tf_op jit(solution)/shard_map/ppermute | solution.py:17
  27.1 7.1 %collective-permute-done.1 = f32[512,16,16]{0,2,1:T(8,128)S(1)} collective-permute-done((f32[512,16,16]{0,2,1:T(8,128)S(1)}, f32[512,16,16]{0,2,1:T(8,128)S(1)}, u32[]{:S(2)}, u32[]{:S(2)}) %collective-permute-start.1) | collective-permute-done | bytes 524320 | tf_op jit(solution)/shard_map/ppermute | solution.py:18
  34.2 3.6 copy.14
  38.2 3.6 copy.12
  41.8 120.8 %fusion.91 = f32[512,16,128]{2,1,0:T(8,128)S(1)} fusion(f32[512,16,128]{2,1,0:T(8,128)} %param.2, f32[512,16,16]{2,1,0:T(8,128)} %copy.14, f32[512,16,16]{2,1,0:T(8,128)} %copy.12, f32[512]{0:T(512)S(1)} %bitcast.138, f32[512]{0:T(512)S(1)} %bitcast.140, f32[512]{0:T(512)S(1)} %bitcast.144, f32[512]{0:T(512)S(1)} %bitcast.146, f32[512]{0:T(512)S(1)} %bitcast.148, ...), kind=kLoop, calls=%fused_computation.207 | loop fusion | flops 101711872 | bytes 9504768 | tf_op jit(solution)/shard_map/add | solution.py:28
  162.6 1.3 collective-permute-start.3
  163.9 3.3 collective-permute-start.2
  167.2 4.4 collective-permute-done.3
  171.7 2.1 collective-permute-done.2
  173.7 28.0 %fusion.4 = f32[512,16,128]{2,1,0:T(8,128)S(1)} fusion(f32[512,16,128]{2,1,0:T(8,128)S(1)} %fusion.91, f32[512,16,128]{2,1,0:T(8,128)S(1)} %collective-permute-done.3, f32[512,16,128]{2,1,0:T(8,128)S(1)} %collective-permute-done.2, f32[512]{0:T(512)S(1)} %bitcast.139, f32[512]{0:T(512)S(1)} %bitcast.141, f32[512]{0:T(512)S(1)} %bitcast.145, ...), kind=kLoop, calls=%fused_computation.120 | loop fusion | flops 99614720 | bytes 16844800 | tf_op jit(solution)/shard_map/add | solution.py:28
  201.7 2.0 copy-done
  203.7 10.7 %fusion.190 = f32[512,512]{1,0:T(8,128)} fusion(f32[512,16,128]{2,1,0:T(8,128)S(1)} %fusion.4), kind=kOutput, calls=%fused_computation.311 | convolution fusion | flops 6442450944 | bytes 5242880 | tf_op jit(solution)/shard_map/dot_general | solution.py:72
  223.4 0.7 multiply_reduce_fusion.53
  232.7 151.3 %all-gather.3.cloned.1.call-done = f32[8192,512]{1,0:T(8,128)} async-done(((f32[512,512]{1,0:T(8,128)}), f32[8192,512]{1,0:T(8,128)}) %all-gather.3.cloned.1.call-update) | async-done | bytes 16777232 | tf_op jit(solution)/shard_map/all_gather | solution.py:75
  384.1 7.9 %reduce_sum.595 = f32[512,512]{1,0:T(8,128)S(1)} reduce(f32[16,512,512]{2,1,0:T(8,128)} %bitcast.89, f32[]{:T(128)} %constant.44.clone.1), dimensions={0}, to_apply=%region_0.0 | reduce | flops 3932160 | bytes 17825796 | tf_op jit(solution)/shard_map/reduce_sum | solution.py:75
  392.0 0.8 select_reduce_fusion
  393.5 1.0 fusion.197
  394.5 0.7 multiply_reduce_fusion.47
  400.7 0.7 multiply_reduce_fusion.42
  404.1 0.7 multiply_reduce_fusion.37
  407.2 0.7 multiply_reduce_fusion.36
  408.6 0.7 multiply_reduce_fusion.35
  410.0 0.7 multiply_reduce_fusion.34
  411.4 0.7 multiply_reduce_fusion.33
  412.8 0.7 multiply_reduce_fusion.32
  414.2 1.2 fusion.195
  415.5 0.7 multiply_reduce_fusion.31
  421.7 0.7 multiply_reduce_fusion.26
  425.1 0.7 multiply_reduce_fusion.21
  428.2 0.7 multiply_reduce_fusion.20
  429.6 0.7 multiply_reduce_fusion.19
  432.4 0.7 multiply_reduce_fusion.17
  433.8 0.7 multiply_reduce_fusion.16
  435.2 1.0 fusion.193
  436.2 0.7 multiply_reduce_fusion.15
  442.5 0.7 multiply_reduce_fusion.10
  445.8 0.7 multiply_reduce_fusion.5
  449.0 0.7 multiply_reduce_fusion.4
  450.4 0.7 multiply_reduce_fusion.3
  453.2 0.7 multiply_reduce_fusion.1
  454.6 0.7 multiply_reduce_fusion
  456.0 5.5 %fusion.180 = f32[4,2048]{1,0:T(4,128)S(1)} fusion(f32[64,8,16,128]{3,2,1,0:T(8,128)} %bitcast.87, f32[512,1]{0,1:T(1,128)S(1)} %divide_multiply_fusion, f32[512,1]{0,1:T(1,128)S(1)} %get-tuple-element.31, f32[512,1]{0,1:T(1,128)S(1)} %get-tuple-element.29, f32[512,1]{0,1:T(1,128)S(1)} %get-tuple-element.46), kind=kOutput, calls=%fused_computation.297 | convolution fusion | flops 50337792 | bytes 4235264 | tf_op jit(solution)/shard_map/dot_general | solution.py:77
  461.5 4.7 fusion.182
  466.3 2.9 copy.20
  (73 shorter events, 19.8 us)
Async XLA Ops:
  6.5 377.5 %all-gather.3.cloned.1.call-start = ((), (), s32[]{:S(2)}) async-start(), calls=%async_computation | async-start | bytes 17825792 | tf_op jit(solution)/shard_map/all_gather | solution.py:75
  14.5 12.6 %copy-start.2 = (f32[512,33]{0,1:T(8,128)S(1)}, f32[512,33]{0,1:T(8,128)}, u32[]{:S(2)}) copy-start(f32[512,33]{0,1:T(8,128)} %param.3) | copy-start | bytes 202756
  17.3 16.9 %collective-permute-start.1 = (f32[512,16,16]{0,2,1:T(8,128)S(1)}, f32[512,16,16]{0,2,1:T(8,128)S(1)}, u32[]{:S(2)}, u32[]{:S(2)}) collective-permute-start(f32[512,16,16]{0,2,1:T(8,128)S(1)} %copy.18), channel_id=1, source_target_pairs={{1,0},{2,1},{3,2},{5,4},{6,5},{7,6},{9,8},{10,9},{11,10},{13,12},{... | collective-permute-start | bytes 1572872 | tf_op jit(solution)/shard_map/ppermute | solution.py:18
  21.4 16.8 %collective-permute-start = (f32[512,16,16]{0,2,1:T(8,128)S(1)}, f32[512,16,16]{0,2,1:T(8,128)S(1)}, u32[]{:S(2)}, u32[]{:S(2)}) collective-permute-start(f32[512,16,16]{0,2,1:T(8,128)S(1)} %copy.17), channel_id=1, source_target_pairs={{0,1},{1,2},{2,3},{4,5},{5,6},{6,7},{8,9},{9,10},{10,11},{12,13},{... | collective-permute-start | bytes 1572872 | tf_op jit(solution)/shard_map/ppermute | solution.py:17
  162.6 9.1 %collective-permute-start.3 = (f32[512,16,128]{2,1,0:T(8,128)S(1)}, f32[512,16,128]{2,1,0:T(8,128)S(1)}, u32[]{:S(2)}, u32[]{:S(2)}) collective-permute-start(f32[512,16,128]{2,1,0:T(8,128)S(1)} %fusion.91), channel_id=1, source_target_pairs={{4,0},{8,4},{12,8},{5,1},{9,5},{13,9},{6,2},{10,6},{14,10},{7,3},{... | collective-permute-start | bytes 12582920 | tf_op jit(solution)/shard_map/ppermute | solution.py:18
  163.9 9.8 %collective-permute-start.2 = (f32[512,16,128]{2,1,0:T(8,128)S(1)}, f32[512,16,128]{2,1,0:T(8,128)S(1)}, u32[]{:S(2)}, u32[]{:S(2)}) collective-permute-start(f32[512,16,128]{2,1,0:T(8,128)S(1)} %fusion.91), channel_id=1, source_target_pairs={{0,4},{4,8},{8,12},{1,5},{5,9},{9,13},{2,6},{6,10},{10,14},{3,7},{... | collective-permute-start | bytes 12582920 | tf_op jit(solution)/shard_map/ppermute | solution.py:17
  201.7 2.0 copy-start
  456.0 5.5 %copy-start.1 = (f32[512,16,128]{2,1,0:T(8,128)S(1)}, f32[512,16,128]{2,1,0:T(8,128)}, u32[]{:S(2)}) copy-start(f32[512,16,128]{2,1,0:T(8,128)} %copy-done) | copy-start | bytes 12582916
Sparse Core Ops, SparseCore 0:
  214.6 169.4 all-gather.2
